TPU v7x, 256 devices: a whole 4x4x8 slice. The times are simulated.
256 devices in a mesh: pre: 16 (over x_lo, z), tp: 8 (over x_hi, y), dec: 2 (over core).
Axes of the slice: x: 4 (x_hi: 2, x_lo: 2; x = x_hi * 2 + x_lo), y: 4, z: 8, core: 2. Of those that a mesh axis runs over, the one named last changes fastest.
Arguments:
- tokens: bfloat16 [16384, 2048], P(('pre', 'tp', 'dec')), may hold values from -6 to 6
- route_ids: int32 [16384, 6], P(('pre', 'tp', 'dec')), may hold values from 0 to 63, all different within a row; in each aligned block of 64 rows (0 to 63, 64 to 127, ...) at most 12 rows name the same one
- route_weights: float32 [16384, 6], P(('pre', 'tp', 'dec')), may hold values from 0.05 to 0.4
- gate_weight: bfloat16 [2048, 90112], P(None, ('pre', 'tp')), may hold values from -0.125 to 0.125
- up_weight: bfloat16 [2048, 90112], P(None, ('pre', 'tp')), may hold values from -0.125 to 0.125
- down_weight: bfloat16 [90112, 2048], P(('pre', 'tp')), may hold values from -0.15625 to 0.15625
- prefill_cache: bfloat16 [2, 8, 256, 64, 1024], P(None, 'tp', 'pre', None, 'dec'), may hold values from -6 to 6
- handover_table: int32 [8, 256], replicated, may hold values from 0 to 255, as said below
Outputs:
- moe_output: bfloat16 [16384, 2048], P(('pre', 'tp', 'dec'))
- decode_cache: bfloat16 [2, 8, 256, 64, 1024], P(None, 'tp', 'pre', None, 'dec')
Inputs may be any that keep to these rules, and one draw needn't show every extreme that they name: `route_ids`: each token names 6 different experts; within the rows of one device (64 consecutive tokens) no expert is named by more than 12 routes, a bound that some block reaches. `handover_table`: each row is a permutation of 0 to 255. The 16 slots g with g // 16 = s (one prefill device) map to at most 2 slots q with q // 16 = p (one decode device), for every s and p, and to exactly 2 for some pair.
All inputs are finite; a program needn't handle non-finite values.
Results may differ from a plain program's by a relative error of at most 0.0085.
Values may be sent and summed in bfloat16 or wider, within the bound.
No kernel may reach another device: no remote copies, remote signals or barrier semaphores. Data moves between devices by JAX's collectives and lax.ppermute only.
A program may use at most 128 MiB of HBM per device.

v0:
```python
import jax
import jax.numpy as jnp
from jax import lax
from jax.sharding import PartitionSpec as P


def slot_ranks(labels, count):
    onehot = (labels[:, None] == jnp.arange(count, dtype=jnp.int32)[None, :]).astype(jnp.int32)
    before = jnp.cumsum(onehot, axis=0) - onehot
    return jnp.sum(before * onehot, axis=1)


def shards(
    tokens,
    route_ids,
    route_weights,
    gate_weight,
    up_weight,
    down_weight,
    prefill_cache,
    handover_table,
):
    tok_dev, width = tokens.shape
    top_count = route_ids.shape[1]
    groups = lax.axis_size("pre") * lax.axis_size("tp")
    experts_all = groups // 2
    most = min(tok_dev, 2 * tok_dev * top_count // experts_all)
    ids_flat = route_ids.reshape(-1)
    positions = slot_ranks(ids_flat, experts_all)
    dest_row = ids_flat * most + positions
    source_rows = jnp.repeat(jnp.arange(tok_dev, dtype=jnp.int32), top_count)
    packed = (
        jnp.zeros((experts_all * most, width), jnp.bfloat16).at[dest_row].set(tokens[source_rows])
    )
    outgoing = jnp.broadcast_to(
        packed.reshape(experts_all, 1, most, width), (experts_all, 2, most, width)
    )
    outgoing = outgoing.reshape(groups, most, width)
    received = lax.all_to_all(outgoing, ("pre", "tp"), split_axis=0, concat_axis=0, tiled=True)
    flat = received.reshape(-1, width)
    gate = jnp.dot(flat, gate_weight, preferred_element_type=jnp.float32)
    upper = jnp.dot(flat, up_weight, preferred_element_type=jnp.float32)
    hidden = (jax.nn.silu(gate) * upper).astype(jnp.bfloat16)
    result = jnp.dot(hidden, down_weight, preferred_element_type=jnp.float32)
    partial_out = result.reshape(received.shape[0], received.shape[1], width)
    returned = lax.all_to_all(partial_out, ("pre", "tp"), split_axis=0, concat_axis=0, tiled=True)
    expert_rows = jnp.sum(returned.reshape(experts_all, 2, most, width), axis=1).astype(
        jnp.bfloat16
    )
    picked = expert_rows.reshape(-1, width)[dest_row].reshape(tok_dev, top_count, width)
    moe_output = jnp.einsum("tk,tkd->td", route_weights, picked.astype(jnp.float32)).astype(
        jnp.bfloat16
    )
    layers, _, blk_dev, blk, half_width = prefill_cache.shape
    sources = lax.axis_size("pre")
    spare = blk_dev // sources + 1
    column = lax.dynamic_index_in_dim(handover_table, lax.axis_index("tp"), 0, keepdims=False)
    dest_dev = (column // blk_dev).reshape(sources, blk_dev)
    onehot = (dest_dev[:, :, None] == jnp.arange(sources, dtype=jnp.int32)[None, None, :]).astype(
        jnp.int32
    )
    rank_all = jnp.sum((jnp.cumsum(onehot, axis=1) - onehot) * onehot, axis=2)
    here = lax.axis_index("pre")
    my_dest = lax.dynamic_index_in_dim(dest_dev, here, 0, keepdims=False)
    my_rank = lax.dynamic_index_in_dim(rank_all, here, 0, keepdims=False)
    blocks_out = jnp.zeros((layers, sources, spare, blk, half_width), jnp.bfloat16)
    blocks_out = blocks_out.at[:, my_dest, my_rank].set(prefill_cache[:, 0])
    arrived = lax.all_to_all(blocks_out, "pre", split_axis=1, concat_axis=1, tiled=True)
    pool_size = column.shape[0]
    inverse = (
        jnp.zeros((pool_size,), jnp.int32).at[column].set(jnp.arange(pool_size, dtype=jnp.int32))
    )
    anchor = lax.dynamic_slice_in_dim(inverse, here * blk_dev, blk_dev)
    pick = anchor // blk_dev * spare + rank_all.reshape(-1)[anchor]
    decode_cache = arrived.reshape(layers, sources * spare, blk, half_width)[:, pick][:, None]
    return (moe_output, decode_cache)


def solution(mesh):
    return jax.shard_map(
        shards,
        mesh=mesh,
        in_specs=(
            P(("pre", "tp", "dec"), None),
            P(("pre", "tp", "dec"), None),
            P(("pre", "tp", "dec"), None),
            P(None, ("pre", "tp")),
            P(None, ("pre", "tp")),
            P(("pre", "tp"), None),
            P(None, "tp", "pre", None, "dec"),
            P(),
        ),
        out_specs=(P(("pre", "tp", "dec"), None), P(None, "tp", "pre", None, "dec")),
        check_vma=False,
    )
```

profile of v0, /device:TPU:96, one launch (start us, length us, event | category | flops | bytes accessed | tf_op | source)
XLA Modules:
  0.0 748.9 jit_solution(11944358911356710262)
XLA Ops:
  0.6 0.8 broadcast_multiply_fusion
  1.5 0.8 copy.28
  2.8 0.9 reduce-window.6
  4.3 10.4 %scatter_custom_fusion = bf16[768,2048]{1,0:T(8,128)(2,1)} fusion(s32[384]{0:T(512)S(1)} %fusion.13, bf16[64,2048]{1,0:T(8,128)(2,1)} %param.8, s32[1024]{0:T(1024)S(1)} %pad_clamp_fusion.3, bf16[]{:T(256)} %constant.63.clone.1), kind=kCustom, calls=%fused_computation.9 | custom fusion | bytes 3146240 | tf_op jit(solution)/shard_map/scatter | solution.py:33
  14.7 6.1 broadcast_in_dim.35
  20.8 6.7 broadcast_in_dim.36
  27.5 14.6 %all-to-all-start = ((bf16[128,12,2048]{2,1,0:T(8,128)(2,1)}), bf16[128,12,2048]{2,1,0:T(8,128)(2,1)}, u32[]{:S(2)}, u32[]{:S(2)}) async-start(bf16[128,12,2048]{2,1,0:T(8,128)(2,1)} %bitcast.56), calls=%async_computation | async-start | bytes 16777216 | tf_op jit(solution)/shard_map/all_to_all | solution.py:39
  42.1 0.7 fusion.20
  43.0 3.1 copy.32
  46.8 2.4 broadcast_in_dim.37
  49.3 6.0 scatter_fusion
  55.3 4.6 copy.33
  59.9 168.8 %all-to-all-done = bf16[128,12,2048]{2,1,0:T(8,128)(2,1)} async-done(((bf16[128,12,2048]{2,1,0:T(8,128)(2,1)}), bf16[128,12,2048]{2,1,0:T(8,128)(2,1)}, u32[]{:S(2)}, u32[]{:S(2)}) %all-to-all-start) | async-done | bytes 6291488 | tf_op jit(solution)/shard_map/all_to_all | solution.py:39
  228.8 5.7 all-to-all-start.2
  234.5 10.7 %reshape.224 = bf16[1536,2048]{1,0:T(8,128)(2,1)} reshape(bf16[128,12,2048]{2,1,0:T(8,128)(2,1)} %all-to-all-done) | data formatting | bytes 12582912 | tf_op jit(solution)/shard_map/reshape | solution.py:40
  245.2 10.3 %fusion.23 = f32[1536,704]{0,1:T(8,128)} fusion(bf16[1536,2048]{1,0:T(8,128)(2,1)} %reshape.224, bf16[2048,704]{0,1:T(8,128)(2,1)} %param.11), kind=kOutput, calls=%fused_computation.67 | convolution fusion | flops 4429185024 | bytes 13500416 | tf_op jit(solution)/shard_map/dot_general | solution.py:41
  255.5 19.1 %fusion.4 = f32[1536,2048]{1,0:T(8,128)} fusion(bf16[704,2048]{1,0:T(8,128)(2,1)S(1)} %copy-done, f32[1536,704]{0,1:T(8,128)} %fusion.23, bf16[1536,2048]{1,0:T(8,128)(2,1)} %reshape.224, bf16[2048,704]{0,1:T(8,128)(2,1)} %param.12), kind=kOutput, calls=%fused_computation.14 | convolution fusion | flops 8864858112 | bytes 28966912 | tf_op jit(solution)/shard_map/dot_general | solution.py:44
  274.6 14.9 %reshape.225 = f32[128,12,2048]{2,1,0:T(8,128)} reshape(f32[1536,2048]{1,0:T(8,128)} %fusion.4) | data formatting | bytes 25165824 | tf_op jit(solution)/shard_map/reshape | solution.py:45
  289.5 38.4 %all-to-all-done.2 = bf16[2,16,2,64,512]{4,3,2,0,1:T(8,128)(2,1)} async-done(((bf16[2,16,2,64,512]{4,3,2,0,1:T(8,128)(2,1)}), bf16[2,16,2,64,512]{4,3,2,0,1:T(8,128)(2,1)}, u32[]{:S(2)}, u32[]{:S(2)}) %all-to-all-start.2) | async-done | bytes 4194336 | tf_op jit(solution)/shard_map/all_to_all | solution.py:68
  327.9 13.0 %all-to-all-start.1 = ((f32[128,12,2048]{2,1,0:T(8,128)}), f32[128,12,2048]{2,1,0:T(8,128)}, u32[]{:S(2)}, u32[]{:S(2)}) async-start(f32[128,12,2048]{2,1,0:T(8,128)} %reshape.225), calls=%async_computation.1 | async-start | bytes 33554432 | tf_op jit(solution)/shard_map/all_to_all | solution.py:46
  341.2 0.7 compare_select_fusion.2
  341.9 1.4 scatter_custom_fusion.2
  344.2 4.6 copy.34
  348.8 2.9 gather_fusion.2
  351.7 1.5 copy.36
  353.2 365.6 %all-to-all-done.1 = f32[128,12,2048]{2,1,0:T(8,128)} async-done(((f32[128,12,2048]{2,1,0:T(8,128)}), f32[128,12,2048]{2,1,0:T(8,128)}, u32[]{:S(2)}, u32[]{:S(2)}) %all-to-all-start.1) | async-done | bytes 12582944 | tf_op jit(solution)/shard_map/all_to_all | solution.py:46
  718.8 9.6 %bitcast_reduce_fusion = bf16[64,12,2048]{2,1,0:T(8,128)(2,1)} fusion(f32[128,12,2048]{2,1,0:T(8,128)} %all-to-all-done.1), kind=kLoop, calls=%fused_computation.7 | loop fusion | flops 1572864 | bytes 15728640 | tf_op jit(solution)/shard_map/reduce_sum | solution.py:47
  728.4 6.2 convert_element_type.28
  734.5 7.5 %gather_fusion = bf16[384,2048]{1,0:T(8,128)(2,1)} fusion(bf16[768,2048]{1,0:T(8,128)(2,1)} %convert_element_type.28, s32[1024]{0:T(1024)S(1)} %pad_clamp_fusion.2), kind=kCustom, calls=%fused_computation.1 | custom fusion | bytes 3147264 | tf_op jit(solution)/shard_map/gather | solution.py:50
  742.0 3.7 reshape.227
  745.7 2.3 fusion.24
  748.0 0.9 copy.42
  (35 shorter events, 3.1 us)
Async XLA Ops:
  0.6 254.8 %copy-start = (bf16[704,2048]{1,0:T(8,128)(2,1)S(1)}, bf16[704,2048]{1,0:T(8,128)(2,1)}, u32[]{:S(2)}) copy-start(bf16[704,2048]{1,0:T(8,128)(2,1)} %param.13) | copy-start | bytes 8650756
  27.5 201.3 %all-to-all-start = ((bf16[128,12,2048]{2,1,0:T(8,128)(2,1)}), bf16[128,12,2048]{2,1,0:T(8,128)(2,1)}, u32[]{:S(2)}, u32[]{:S(2)}) async-start(bf16[128,12,2048]{2,1,0:T(8,128)(2,1)} %bitcast.56), calls=%async_computation | async-start | bytes 16777216 | tf_op jit(solution)/shard_map/all_to_all | solution.py:39
  228.8 99.1 %all-to-all-start.2 = ((bf16[2,16,2,64,512]{4,3,2,0,1:T(8,128)(2,1)}), bf16[2,16,2,64,512]{4,3,2,0,1:T(8,128)(2,1)}, u32[]{:S(2)}, u32[]{:S(2)}) async-start(bf16[2,16,2,64,512]{4,3,2,0,1:T(8,128)(2,1)} %copy.33), calls=%async_computation.2 | async-start | bytes 8388608 | tf_op jit(solution)/shard_map/all_to_all | solution.py:68
  289.5 51.5 %copy-start.2 = (f32[64,6]{0,1:T(8,128)S(1)}, f32[64,6]{0,1:T(8,128)}, u32[]{:S(2)}) copy-start(f32[64,6]{0,1:T(8,128)} %param.10) | copy-start | bytes 4612
  327.9 390.9 %all-to-all-start.1 = ((f32[128,12,2048]{2,1,0:T(8,128)}), f32[128,12,2048]{2,1,0:T(8,128)}, u32[]{:S(2)}, u32[]{:S(2)}) async-start(f32[128,12,2048]{2,1,0:T(8,128)} %reshape.225), calls=%async_computation.1 | async-start | bytes 33554432 | tf_op jit(solution)/shard_map/all_to_all | solution.py:46
  734.5 14.3 %copy-start.1 = (bf16[704,2048]{1,0:T(8,128)(2,1)S(1)}, bf16[704,2048]{1,0:T(8,128)(2,1)}, u32[]{:S(2)}) copy-start(bf16[704,2048]{1,0:T(8,128)(2,1)} %param.13) | copy-start | bytes 8650756
where the time goes:
time: 751 us; the launch traced here: 749 us
  waiting for transfers between devices  573 us (76%)
  local copies, waits for them, and re-layouts  97.3 us (13%)
  starting transfers between devices  33.4 us (4%)
  matrix products  31.7 us (4%)
  other arithmetic  12.9 us (2%)
    all_to_all x1, waiting for transfers between devices, shards(): lax.all_to_all(partial_out, ('pre', 'tp'), split_axis=0, concat_axis=0, t...  366 us
    all_to_all x1, waiting for transfers between devices, shards(): lax.all_to_all(outgoing, ('pre', 'tp'), split_axis=0, concat_axis=0, tile...  169 us
    all_to_all x1, waiting for transfers between devices, shards(): lax.all_to_all(blocks_out, 'pre', split_axis=1, concat_axis=1, tiled=True)  38.4 us
    dot_general x1, matrix products, shards(): result = jnp.dot(hidden, down_weight, preferred_element_type=jnp.float32)  19.1 us
  transfers between devices with their start and end apart: 3, of which 3 were waited for; matrix products, arithmetic and copies ran while one was open for 11% of the time, Pallas kernels for 0%

commit v1 on v0

--- a/solution.py
+++ b/solution.py
@@ -65,7 +65,10 @@
     my_rank = lax.dynamic_index_in_dim(rank_all, here, 0, keepdims=False)
     blocks_out = jnp.zeros((layers, sources, spare, blk, half_width), jnp.bfloat16)
     blocks_out = blocks_out.at[:, my_dest, my_rank].set(prefill_cache[:, 0])
-    arrived = lax.all_to_all(blocks_out, "pre", split_axis=1, concat_axis=1, tiled=True)
+    size = lax.axis_size("pre")
+    blocks = jnp.stack(jnp.split(blocks_out, size, axis=1), axis=0)
+    blocks = lax.all_to_all(blocks, "pre", split_axis=0, concat_axis=0)
+    arrived = jnp.concatenate(blocks, axis=1)
     pool_size = column.shape[0]
     inverse = (
         jnp.zeros((pool_size,), jnp.int32).at[column].set(jnp.arange(pool_size, dtype=jnp.int32))

time: 751 us -> 751 us (level)
  waiting for transfers between devices: 573 us -> 551 us
  local copies, waits for them, and re-layouts: 97.3 us -> 119 us
    unnamed x9 -> x24, local copies, waits for them, and re-layouts: 2.48 us -> 27.6 us
    all_to_all x1, waiting for transfers between devices: 169 us -> 147 us  [shards(): lax.all_to_all(outgoing, ('pre', 'tp'), split_axis=0, concat_axis=0, tile...]
  transfers between devices with their start and end apart: 3 -> 3, of which waited for: 3 -> 3; matrix products, arithmetic and copies ran while one was open for 11% -> 14% of each run, Pallas kernels for 0% -> 0%
where the time goes in v1:
time: 751 us; the launch traced here: 749 us
  waiting for transfers between devices  551 us (73%)
  local copies, waits for them, and re-layouts  119 us (16%)
  starting transfers between devices  33.4 us (4%)
  matrix products  31.7 us (4%)
  other arithmetic  12.9 us (2%)
    all_to_all x1, waiting for transfers between devices, shards(): lax.all_to_all(partial_out, ('pre', 'tp'), split_axis=0, concat_axis=0, t...  366 us
    all_to_all x1, waiting for transfers between devices, shards(): lax.all_to_all(outgoing, ('pre', 'tp'), split_axis=0, concat_axis=0, tile...  147 us
    all_to_all x1, waiting for transfers between devices, shards(): blocks = lax.all_to_all(blocks, 'pre', split_axis=0, concat_axis=0)  38.4 us
    unnamed x24, local copies, waits for them, and re-layouts  27.6 us
    dot_general x1, matrix products, shards(): result = jnp.dot(hidden, down_weight, preferred_element_type=jnp.float32)  19.1 us
  transfers between devices with their start and end apart: 3, of which 3 were waited for; matrix products, arithmetic and copies ran while one was open for 14% of the time, Pallas kernels for 0%

profile of v1, /device:TPU:96, one launch (start us, length us, event | category | flops | bytes accessed | tf_op | source)
XLA Modules:
  0.0 748.9 jit_solution(7959480846501764847)
XLA Ops:
  4.3 10.4 %scatter_custom_fusion = bf16[768,2048]{1,0:T(8,128)(2,1)} fusion(s32[384]{0:T(512)S(1)} %fusion.29, bf16[64,2048]{1,0:T(8,128)(2,1)} %param.8, s32[1024]{0:T(1024)S(1)} %pad_clamp_fusion.3, bf16[]{:T(256)} %constant.63.clone.1), kind=kCustom, calls=%fused_computation.9 | custom fusion | bytes 3146240 | tf_op jit(solution)/shard_map/scatter | solution.py:33
  14.7 6.1 broadcast_in_dim.35
  20.8 6.7 broadcast_in_dim.36
  27.5 14.6 %all-to-all-start = ((bf16[128,12,2048]{2,1,0:T(8,128)(2,1)}), bf16[128,12,2048]{2,1,0:T(8,128)(2,1)}, u32[]{:S(2)}, u32[]{:S(2)}) async-start(bf16[128,12,2048]{2,1,0:T(8,128)(2,1)} %bitcast.151), calls=%async_computation | async-start | bytes 16777216 | tf_op jit(solution)/shard_map/all_to_all | solution.py:39
  43.0 3.1 copy.77
  46.8 2.4 broadcast_in_dim.37
  49.3 6.0 scatter_fusion
  55.3 1.7 fusion.20
  57.0 1.7 fusion.19
  58.7 1.7 fusion.18
  60.3 1.7 fusion.17
  67.0 1.7 fusion.13
  68.7 1.7 fusion.12
  70.3 1.7 fusion.11
  72.0 1.7 fusion.10
  75.4 1.7 fusion.8
  82.1 146.7 %all-to-all-done = bf16[128,12,2048]{2,1,0:T(8,128)(2,1)} async-done(((bf16[128,12,2048]{2,1,0:T(8,128)(2,1)}), bf16[128,12,2048]{2,1,0:T(8,128)(2,1)}, u32[]{:S(2)}, u32[]{:S(2)}) %all-to-all-start) | async-done | bytes 6291488 | tf_op jit(solution)/shard_map/all_to_all | solution.py:39
  228.8 5.7 all-to-all-start.2
  234.5 10.7 %reshape.224 = bf16[1536,2048]{1,0:T(8,128)(2,1)} reshape(bf16[128,12,2048]{2,1,0:T(8,128)(2,1)} %all-to-all-done) | data formatting | bytes 12582912 | tf_op jit(solution)/shard_map/reshape | solution.py:40
  245.2 10.3 %fusion.39 = f32[1536,704]{0,1:T(8,128)} fusion(bf16[1536,2048]{1,0:T(8,128)(2,1)} %reshape.224, bf16[2048,704]{0,1:T(8,128)(2,1)} %param.11), kind=kOutput, calls=%fused_computation.99 | convolution fusion | flops 4429185024 | bytes 13500416 | tf_op jit(solution)/shard_map/dot_general | solution.py:41
  255.5 19.1 %fusion.4 = f32[1536,2048]{1,0:T(8,128)} fusion(bf16[704,2048]{1,0:T(8,128)(2,1)S(1)} %copy-done, f32[1536,704]{0,1:T(8,128)} %fusion.39, bf16[1536,2048]{1,0:T(8,128)(2,1)} %reshape.224, bf16[2048,704]{0,1:T(8,128)(2,1)} %param.12), kind=kOutput, calls=%fused_computation.14 | convolution fusion | flops 8864858112 | bytes 28966912 | tf_op jit(solution)/shard_map/dot_general | solution.py:44
  274.6 14.9 %reshape.225 = f32[128,12,2048]{2,1,0:T(8,128)} reshape(f32[1536,2048]{1,0:T(8,128)} %fusion.4) | data formatting | bytes 25165824 | tf_op jit(solution)/shard_map/reshape | solution.py:45
  289.5 38.4 %all-to-all-done.2 = bf16[16,2,1,2,64,512]{5,4,3,1,2,0:T(8,128)(2,1)} async-done(((bf16[16,2,1,2,64,512]{5,4,3,1,2,0:T(8,128)(2,1)}), bf16[16,2,1,2,64,512]{5,4,3,1,2,0:T(8,128)(2,1)}, u32[]{:S(2)}, u32[]{:S(2)}) %all-to-all-start.2) | async-done | bytes 4194336 | tf_op jit(solution)/shard_map/all_to_all | solution.py:70
  327.9 13.0 %all-to-all-start.1 = ((f32[128,12,2048]{2,1,0:T(8,128)}), f32[128,12,2048]{2,1,0:T(8,128)}, u32[]{:S(2)}, u32[]{:S(2)}) async-start(f32[128,12,2048]{2,1,0:T(8,128)} %reshape.225), calls=%async_computation.1 | async-start | bytes 33554432 | tf_op jit(solution)/shard_map/all_to_all | solution.py:46
  344.2 4.6 copy.93
  348.8 2.9 gather_fusion.2
  353.2 365.6 %all-to-all-done.1 = f32[128,12,2048]{2,1,0:T(8,128)} async-done(((f32[128,12,2048]{2,1,0:T(8,128)}), f32[128,12,2048]{2,1,0:T(8,128)}, u32[]{:S(2)}, u32[]{:S(2)}) %all-to-all-start.1) | async-done | bytes 12582944 | tf_op jit(solution)/shard_map/all_to_all | solution.py:46
  718.8 9.6 %bitcast_reduce_fusion = bf16[64,12,2048]{2,1,0:T(8,128)(2,1)} fusion(f32[128,12,2048]{2,1,0:T(8,128)} %all-to-all-done.1), kind=kLoop, calls=%fused_computation.7 | loop fusion | flops 1572864 | bytes 15728640 | tf_op jit(solution)/shard_map/reduce_sum | solution.py:47
  728.4 6.2 convert_element_type.28
  734.5 7.5 %gather_fusion = bf16[384,2048]{1,0:T(8,128)(2,1)} fusion(bf16[768,2048]{1,0:T(8,128)(2,1)} %convert_element_type.28, s32[1024]{0:T(1024)S(1)} %pad_clamp_fusion.2), kind=kCustom, calls=%fused_computation.1 | custom fusion | bytes 3147264 | tf_op jit(solution)/shard_map/gather | solution.py:50
  742.0 3.7 reshape.227
  745.7 2.3 fusion.40
  (50 shorter events, 22.5 us)
Async XLA Ops:
  0.6 254.8 %copy-start = (bf16[704,2048]{1,0:T(8,128)(2,1)S(1)}, bf16[704,2048]{1,0:T(8,128)(2,1)}, u32[]{:S(2)}) copy-start(bf16[704,2048]{1,0:T(8,128)(2,1)} %param.13) | copy-start | bytes 8650756
  27.5 201.3 %all-to-all-start = ((bf16[128,12,2048]{2,1,0:T(8,128)(2,1)}), bf16[128,12,2048]{2,1,0:T(8,128)(2,1)}, u32[]{:S(2)}, u32[]{:S(2)}) async-start(bf16[128,12,2048]{2,1,0:T(8,128)(2,1)} %bitcast.151), calls=%async_computation | async-start | bytes 16777216 | tf_op jit(solution)/shard_map/all_to_all | solution.py:39
  228.8 99.1 %all-to-all-start.2 = ((bf16[16,2,1,2,64,512]{5,4,3,1,2,0:T(8,128)(2,1)}), bf16[16,2,1,2,64,512]{5,4,3,1,2,0:T(8,128)(2,1)}, u32[]{:S(2)}, u32[]{:S(2)}) async-start(bf16[16,2,1,2,64,512]{5,4,3,1,2,0:T(8,128)(2,1)} %fusion.5), calls=%async_computation.2 | async-start | bytes 8388608 | tf_op jit(solution)/shard_map/all_to_all | solution.py:70
  289.5 51.5 %copy-start.2 = (f32[64,6]{0,1:T(8,128)S(1)}, f32[64,6]{0,1:T(8,128)}, u32[]{:S(2)}) copy-start(f32[64,6]{0,1:T(8,128)} %param.10) | copy-start | bytes 4612
  327.9 390.9 %all-to-all-start.1 = ((f32[128,12,2048]{2,1,0:T(8,128)}), f32[128,12,2048]{2,1,0:T(8,128)}, u32[]{:S(2)}, u32[]{:S(2)}) async-start(f32[128,12,2048]{2,1,0:T(8,128)} %reshape.225), calls=%async_computation.1 | async-start | bytes 33554432 | tf_op jit(solution)/shard_map/all_to_all | solution.py:46
  734.5 14.3 %copy-start.1 = (bf16[704,2048]{1,0:T(8,128)(2,1)S(1)}, bf16[704,2048]{1,0:T(8,128)(2,1)}, u32[]{:S(2)}) copy-start(bf16[704,2048]{1,0:T(8,128)(2,1)} %param.13) | copy-start | bytes 8650756
